TPU v7x, 128 devices: a whole 4x4x4 slice. The times are simulated.
128 devices in a mesh: dom: 128 (over x, y, z, core).
Axes of the slice: x: 4, y: 4, z: 4, core: 2. Of those that a mesh axis runs over, the one named last changes fastest.
Arguments:
- traction: float32 [65536, 3, 128], P('dom'), may hold values from -6 to 6
- fluid_coords: float32 [65536, 3, 128], P('dom'), may hold values from 0 to 1
- struct_coords: float32 [3, 32, 16384], P(None, None, 'dom'), may hold values from 0 to 1
- dest: int32 [65536, 1], P('dom'), may hold values from 0 to 127; in each aligned block of 512 rows (0 to 511, 512 to 1023, ...) at most 8 rows name the same one
- target: int32 [65536], P('dom'), may hold values from 0 to 127
- blocks: float32 [3, 96, 96, 16384], P(None, None, None, 'dom'), may hold values from -1 to 7, as said below
- columns: int32 [2, 16384], P(None, 'dom'), may hold values from 0 to 159
- halo_list: int32 [2048], P('dom'), may hold values from 0 to 127
- precond: float32 [96, 96, 16384], P(None, None, 'dom'), may hold values from -1 to 1
Outputs:
- load_field: float32 [96, 16384], P(None, 'dom')
- solution: float32 [96, 16384], P(None, 'dom')
- residual: float32 [96, 16384], P(None, 'dom')
Inputs may be any that keep to these rules, and one draw needn't show every extreme that they name: `dest`: among the fluid blocks of one partition no partition is named more than 8 times, a bound that some block reaches. Each diagonal block is its positive diagonal plus small full entries; coupling blocks are small full blocks.
All inputs are finite; a program needn't handle non-finite values.
Results may differ from a plain program's by a relative error of at most 0.0003.
Values sent between devices are 32-bit elements; how exact they have to be, the bound alone decides.
No kernel may reach another device: no remote copies, remote signals or barrier semaphores. Data moves between devices by JAX's collectives and lax.ppermute only.
A program may use at most 128 MiB of HBM per device.

v0:
```python
import jax
import jax.numpy as jnp
from jax import lax
from jax.sharding import Mesh
from jax.sharding import PartitionSpec as P

ITERS = 2
DOM = ("dom_0", "dom_1", "dom_2", "dom_3")
support = 0.9


def from_behind(block, axis, distance):
    devices = range(lax.axis_size(axis))
    route = [(i - distance, i) for i in devices if i - distance in devices]
    return lax.ppermute(block, axis, route)


def over_axes(shard, axes):
    for axis in axes:
        shard = lax.psum(shard, axis)
    return shard


def wendland_map(fluid_pos, force, struct_pos):
    dist_sq = jnp.zeros((fluid_pos.shape[0], struct_pos.shape[2], fluid_pos.shape[2]), jnp.float32)
    for component in range(3):
        dist_sq = (
            dist_sq + (struct_pos[:, component, :, None] - fluid_pos[:, component, None, :]) ** 2
        )
    radius = jnp.sqrt(dist_sq) / support
    weight = jnp.maximum(1.0 - radius, 0.0) ** 4 * (4.0 * radius + 1.0)
    mapped = jnp.einsum("bjn,bcn->bcj", weight, force, precision=lax.Precision.HIGHEST)
    return mapped.reshape(mapped.shape[0], -1)


def precondition(precond, vector):
    return jnp.einsum("abi,bi->ai", precond, vector, precision=lax.Precision.HIGHEST)


def apply_operator(vector, blocks, columns, halo_list):
    outgoing = jnp.take(vector, halo_list, axis=1)
    from_left = from_behind(outgoing, DOM, 1)
    from_right = from_behind(outgoing, DOM, -1)
    extended = jnp.concatenate([vector, from_left, from_right], axis=1)
    result = jnp.einsum("abi,bi->ai", blocks[0], vector, precision=lax.Precision.HIGHEST)
    for neighbor in range(columns.shape[0]):
        taken = jnp.take(extended, columns[neighbor], axis=1)
        result = result + jnp.einsum(
            "abi,bi->ai", blocks[neighbor + 1], taken, precision=lax.Precision.HIGHEST
        )
    return result


def on_device(
    traction, fluid_coords, struct_coords, dest, target, blocks, columns, halo_list, precond
):
    partitions = lax.axis_size(DOM)
    fluid_count = dest.shape[0]
    node_count = traction.shape[2]
    cluster = blocks.shape[1]
    local_blocks = blocks.shape[3]
    capacity = max(2, 2 * fluid_count // partitions)
    owner_part = dest[:, 0]
    owner_hits = (owner_part[:, None] == jnp.arange(partitions, dtype=jnp.int32)[None, :]).astype(
        jnp.int32
    )
    before = jnp.sum((jnp.cumsum(owner_hits, axis=0) - owner_hits) * owner_hits, axis=1)
    slot_index = owner_part * capacity + before
    slot_target = jnp.zeros((partitions * capacity,), jnp.int32).at[slot_index].set(target)
    slot_target = slot_target.reshape(partitions, capacity)
    packed = jnp.concatenate([traction, fluid_coords], axis=1)
    outgoing = (
        jnp.zeros((partitions * capacity, 6, node_count), jnp.float32).at[slot_index].set(packed)
    )
    outgoing = outgoing.reshape(partitions, capacity, 6, node_count)
    floats = lax.all_to_all(outgoing, DOM, split_axis=0, concat_axis=0, tiled=True)
    labels = lax.all_to_all(slot_target, DOM, split_axis=0, concat_axis=0, tiled=True)
    item_count = floats.shape[1]
    flattened = floats.reshape(partitions * item_count, 6, node_count)
    struct_pos = jnp.transpose(jnp.take(struct_coords, labels.reshape(-1), axis=2), (2, 0, 1))
    mapped = wendland_map(flattened[:, 3:], flattened[:, :3], struct_pos)
    arrived, labels = (mapped.reshape(partitions, item_count, cluster), labels)
    onehot = (
        labels.reshape(-1)[:, None] == jnp.arange(local_blocks, dtype=jnp.int32)[None, :]
    ).astype(jnp.float32)
    load_field = jnp.dot(
        arrived.reshape(-1, cluster).T,
        onehot,
        precision=lax.Precision.HIGHEST,
        preferred_element_type=jnp.float32,
    )
    solution = jnp.zeros_like(load_field)
    residual = load_field
    search = load_field
    alignment = over_axes(jnp.sum(load_field * residual), DOM)
    for step in range(ITERS):
        search_pre = precondition(precond, search)
        image = apply_operator(search_pre, blocks, columns, halo_list)
        step_size = alignment / over_axes(jnp.sum(load_field * image), DOM)
        middle = residual - step_size * image
        middle_pre = precondition(precond, middle)
        middle_image = apply_operator(middle_pre, blocks, columns, halo_list)
        crossed, squared, with_middle, with_image = (
            over_axes(jnp.sum(middle_image * middle), DOM),
            over_axes(jnp.sum(middle_image * middle_image), DOM),
            over_axes(jnp.sum(load_field * middle), DOM),
            over_axes(jnp.sum(load_field * middle_image), DOM),
        )
        smoothing = crossed / squared
        solution = solution + step_size * search_pre + smoothing * middle_pre
        residual = middle - smoothing * middle_image
        new_alignment = with_middle - smoothing * with_image
        momentum = new_alignment / alignment * (step_size / smoothing)
        search = residual + momentum * (search - smoothing * image)
        alignment = new_alignment
    return (load_field, solution, residual)


def solution(mesh):
    finer = Mesh(mesh.devices.reshape(4, 4, 4, 2), ("dom_0", "dom_1", "dom_2", "dom_3"))
    in_specs = (
        P(DOM, None, None),
        P(DOM, None, None),
        P(None, None, DOM),
        P(DOM, None),
        P(DOM),
        P(None, None, None, DOM),
        P(None, DOM),
        P(DOM),
        P(None, None, DOM),
    )
    out_specs = (P(None, DOM), P(None, DOM), P(None, DOM))
    return jax.shard_map(
        on_device, mesh=finer, in_specs=in_specs, out_specs=out_specs, check_vma=False
    )
```

profile of v0, /device:TPU:1, one launch (start us, length us, event | category | flops | bytes accessed | tf_op | source)
XLA Modules:
  0.0 407.8 jit_solution(7936706679427344915)
XLA Ops:
  6.7 11.5 %all-to-all-start.1 = ((s32[128,1,8]{2,1,0:T(1,128)}), s32[128,1,8]{2,1,0:T(1,128)S(1)}, u32[]{:S(2)}, u32[]{:S(2)}) async-start(s32[128,1,8]{2,1,0:T(1,128)} %bitcast.41), calls=%async_computation.1 | async-start | bytes 131072 | tf_op jit(solution)/shard_map/all_to_all | solution.py:77
  22.8 47.3 %scatter_fusion = f32[1024,6,128]{2,1,0:T(8,128)} fusion(f32[1024,6,128]{2,1,0:T(8,128)} %broadcast_in_dim.40, s32[512]{0:T(512)S(1)} %bitcast.249, f32[512,6,128]{2,1,0:T(8,128)S(1)} %copy.103), kind=kCustom, calls=%fused_computation.13 | custom fusion | bytes 4720640 | tf_op jit(solution)/shard_map/scatter | solution.py:73
  74.7 9.8 %all-to-all-start = ((f32[128,8,6,128]{3,1,2,0:T(8,128)}), f32[128,8,6,128]{3,1,2,0:T(8,128)S(1)}, u32[]{:S(2)}, u32[]{:S(2)}) async-start(f32[128,8,6,128]{3,1,2,0:T(8,128)} %copy.104), calls=%async_computation | async-start | bytes 6291456 | tf_op jit(solution)/shard_map/all_to_all | solution.py:76
  87.8 8.0 %gather_fusion = f32[1024,3,32]{2,1,0:T(4,128)} fusion(f32[3,32,128]{1,0,2:T(4,128)S(1)} %copy.107, s32[1024]{0:T(1024)S(1)} %broadcast_clamp_fusion), kind=kCustom, calls=%fused_computation.12 | custom fusion | bytes 790528 | tf_op jit(solution)/shard_map/jit(_take)/gather | solution.py:80
  103.6 22.7 %all-to-all-done = f32[128,8,6,128]{3,1,2,0:T(8,128)S(1)} async-done(((f32[128,8,6,128]{3,1,2,0:T(8,128)}), f32[128,8,6,128]{3,1,2,0:T(8,128)S(1)}, u32[]{:S(2)}, u32[]{:S(2)}) %all-to-all-start) | async-done | bytes 3145760 | tf_op jit(solution)/shard_map/all_to_all | solution.py:76
  128.5 42.6 %fusion = f32[1024,3,32]{2,1,0:T(4,128)S(1)} fusion(f32[1024,128]{1,0:T(8,128)S(1)} %bitcast.242, f32[1024,32]{1,0:T(8,128)S(1)} %bitcast.240, f32[1024,128]{1,0:T(8,128)S(1)} %bitcast.243, f32[1024,32]{1,0:T(8,128)S(1)} %bitcast.239, f32[1024,128]{1,0:T(8,128)S(1)} %bitcast.241, f32[1024,32]{1,0:T(8,128)S(1)} %bitcast.238, f32[1024,6,128]{2,1,0:T(8,128)S(1)} %bitcast.223), kind=kOutput, calls=%fused_computation.15 | convolution fusion | flops 218103808 | bytes 5636096 | tf_op jit(solution)/shard_map/bjn,bcn->bcj/dot_general | solution.py:32
  184.4 6.2 %fusion.32 = (f32[128,96]{0,1:T(8,128)S(1)}, f32[128,96]{0,1:T(8,128)S(1)}, f32[128,96]{0,1:T(8,128)S(1)}) fusion(f32[3,96,96,128]{3,2,1,0:T(8,128)} %param.18, f32[128,96]{0,1:T(8,128)S(1)} %copy.236, f32[128,96]{0,1:T(8,128)S(1)} %multiply_reduce_fusion.3, f32[128,96]{0,1:T(8,128)S(1)} %copy.237), kind=kLoop, calls=%fused_computation.55 | loop fusion | flops 7041024 | bytes 14450688 | tf_op jit(solution)/shard_map/abi,bi->ai/dot_general | solution.py:48
  191.2 8.0 %all-reduce.8 = (f32[]{:T(128)}, f32[]{:T(128)}) all-reduce(f32[]{:T(128)} %get-tuple-element.24, f32[]{:T(128)} %get-tuple-element.23), channel_id=1, replica_groups=mesh['dom_0'=4,'dom_1'=4,'dom_2'=4,'dom_3'=2] {'dom_0'}, use_global_device_ids=true, to_apply=%region_6.7 | all-reduce | flops 2 | bytes 16 | tf_op jit(solution)/shard_map/psum | solution.py:20
  199.2 6.7 %all-reduce.5 = (f32[]{:T(128)}, f32[]{:T(128)}) all-reduce(f32[]{:T(128)} %get-tuple-element.47, f32[]{:T(128)} %get-tuple-element.48), channel_id=1, replica_groups=mesh['dom_0'=4,'dom_1'=4,'dom_2'=4,'dom_3'=2] {'dom_1'}, use_global_device_ids=true, to_apply=%region_7.8 | all-reduce | flops 2 | bytes 16 | tf_op jit(solution)/shard_map/psum | solution.py:20
  205.9 11.0 %all-reduce.2 = (f32[]{:T(128)}, f32[]{:T(128)}) all-reduce(f32[]{:T(128)} %get-tuple-element.39, f32[]{:T(128)} %get-tuple-element.40), channel_id=1, replica_groups=mesh['dom_0'=4,'dom_1'=4,'dom_2'=4,'dom_3'=2] {'dom_2'}, use_global_device_ids=true, to_apply=%region_8.9 | all-reduce | flops 2 | bytes 16 | tf_op jit(solution)/shard_map/psum | solution.py:20
  216.9 10.4 %all-reduce.11 = (f32[]{:T(128)}, f32[]{:T(128)}) all-reduce(f32[]{:T(128)} %get-tuple-element.31, f32[]{:T(128)} %get-tuple-element.32), channel_id=1, replica_groups=mesh['dom_0'=4,'dom_1'=4,'dom_2'=4,'dom_3'=2] {'dom_3'}, use_global_device_ids=true, to_apply=%region_9.10 | all-reduce | flops 2 | bytes 16 | tf_op jit(solution)/shard_map/psum | solution.py:20
  241.0 6.2 %fusion.33 = (f32[128,96]{0,1:T(8,128)S(1)}, f32[128,96]{0,1:T(8,128)S(1)}, f32[128,96]{0,1:T(8,128)S(1)}) fusion(f32[3,96,96,128]{3,2,1,0:T(8,128)} %param.18, f32[128,96]{0,1:T(8,128)S(1)} %copy.241, f32[128,96]{0,1:T(8,128)S(1)} %multiply_reduce_fusion.2, f32[128,96]{0,1:T(8,128)S(1)} %copy.242), kind=kLoop, calls=%fused_computation.56 | loop fusion | flops 7041024 | bytes 14450688 | tf_op jit(solution)/shard_map/abi,bi->ai/dot_general | solution.py:48
  248.0 9.3 %all-reduce.7 = (f32[]{:T(128)}, f32[]{:T(128)}, f32[]{:T(128)}, f32[]{:T(128)}) all-reduce(f32[]{:T(128)} %get-tuple-element.19, f32[]{:T(128)} %get-tuple-element.18, f32[]{:T(128)} %get-tuple-element.22, f32[]{:T(128)} %get-tuple-element.17), channel_id=1, replica_groups=mesh['dom_0'=4,'dom_1'=4,'dom_2'=4,'dom_3'=2] {'dom_0'}, use_global_device_ids=true, to_apply=%region_26.29 | all-reduce | flops 4 | bytes 32 | tf_op jit(solution)/shard_map/psum | solution.py:20
  257.3 6.7 %all-reduce.4 = (f32[]{:T(128)}, f32[]{:T(128)}, f32[]{:T(128)}, f32[]{:T(128)}) all-reduce(f32[]{:T(128)} %get-tuple-element.43, f32[]{:T(128)} %get-tuple-element.44, f32[]{:T(128)} %get-tuple-element.45, f32[]{:T(128)} %get-tuple-element.46), channel_id=1, replica_groups=mesh['dom_0'=4,'dom_1'=4,'dom_2'=4,'dom_3'=2] {'dom_1'}, use_global_device_ids=true, to_apply=%region_27.30 | all-reduce | flops 4 | bytes 32 | tf_op jit(solution)/shard_map/psum | solution.py:20
  264.0 11.5 %all-reduce.1 = (f32[]{:T(128)}, f32[]{:T(128)}, f32[]{:T(128)}, f32[]{:T(128)}) all-reduce(f32[]{:T(128)} %get-tuple-element.35, f32[]{:T(128)} %get-tuple-element.36, f32[]{:T(128)} %get-tuple-element.37, f32[]{:T(128)} %get-tuple-element.38), channel_id=1, replica_groups=mesh['dom_0'=4,'dom_1'=4,'dom_2'=4,'dom_3'=2] {'dom_2'}, use_global_device_ids=true, to_apply=%region_28.31 | all-reduce | flops 4 | bytes 32 | tf_op jit(solution)/shard_map/psum | solution.py:20
  275.5 10.1 %all-reduce.10 = (f32[]{:T(128)}, f32[]{:T(128)}, f32[]{:T(128)}, f32[]{:T(128)}) all-reduce(f32[]{:T(128)} %get-tuple-element.27, f32[]{:T(128)} %get-tuple-element.28, f32[]{:T(128)} %get-tuple-element.29, f32[]{:T(128)} %get-tuple-element.30), channel_id=1, replica_groups=mesh['dom_0'=4,'dom_1'=4,'dom_2'=4,'dom_3'=2] {'dom_3'}, use_global_device_ids=true, to_apply=%region_29.32 | all-reduce | flops 4 | bytes 32 | tf_op jit(solution)/shard_map/psum | solution.py:20
  310.6 9.3 %psum.276 = f32[]{:T(128)} all-reduce(f32[]{:T(128)} %fusion.51), channel_id=1, replica_groups=mesh['dom_0'=4,'dom_1'=4,'dom_2'=4,'dom_3'=2] {'dom_0'}, use_global_device_ids=true, to_apply=%region_36.39 | all-reduce | flops 1 | bytes 8 | tf_op jit(solution)/shard_map/psum | solution.py:20
  319.9 6.6 %psum.277 = f32[]{:T(128)} all-reduce(f32[]{:T(128)} %psum.276), channel_id=1, replica_groups=mesh['dom_0'=4,'dom_1'=4,'dom_2'=4,'dom_3'=2] {'dom_1'}, use_global_device_ids=true, to_apply=%region_37.40 | all-reduce | flops 1 | bytes 8 | tf_op jit(solution)/shard_map/psum | solution.py:20
  326.5 11.4 %psum.278 = f32[]{:T(128)} all-reduce(f32[]{:T(128)} %psum.277), channel_id=1, replica_groups=mesh['dom_0'=4,'dom_1'=4,'dom_2'=4,'dom_3'=2] {'dom_2'}, use_global_device_ids=true, to_apply=%region_38.41 | all-reduce | flops 1 | bytes 8 | tf_op jit(solution)/shard_map/psum | solution.py:20
  337.9 10.0 %psum.279 = f32[]{:T(128)} all-reduce(f32[]{:T(128)} %psum.278), channel_id=1, replica_groups=mesh['dom_0'=4,'dom_1'=4,'dom_2'=4,'dom_3'=2] {'dom_3'}, use_global_device_ids=true, to_apply=%region_39.42 | all-reduce | flops 1 | bytes 8 | tf_op jit(solution)/shard_map/psum | solution.py:20
  367.8 9.3 %all-reduce.6 = (f32[]{:T(128)}, f32[]{:T(128)}) all-reduce(f32[]{:T(128)} %get-tuple-element.21, f32[]{:T(128)} %get-tuple-element.20), channel_id=1, replica_groups=mesh['dom_0'=4,'dom_1'=4,'dom_2'=4,'dom_3'=2] {'dom_0'}, use_global_device_ids=true, to_apply=%region_41.44 | all-reduce | flops 2 | bytes 16 | tf_op jit(solution)/shard_map/psum | solution.py:20
  377.1 6.6 %all-reduce.3 = (f32[]{:T(128)}, f32[]{:T(128)}) all-reduce(f32[]{:T(128)} %get-tuple-element.41, f32[]{:T(128)} %get-tuple-element.42), channel_id=1, replica_groups=mesh['dom_0'=4,'dom_1'=4,'dom_2'=4,'dom_3'=2] {'dom_1'}, use_global_device_ids=true, to_apply=%region_42.45 | all-reduce | flops 2 | bytes 16 | tf_op jit(solution)/shard_map/psum | solution.py:20
  383.7 11.4 %all-reduce = (f32[]{:T(128)}, f32[]{:T(128)}) all-reduce(f32[]{:T(128)} %get-tuple-element.33, f32[]{:T(128)} %get-tuple-element.34), channel_id=1, replica_groups=mesh['dom_0'=4,'dom_1'=4,'dom_2'=4,'dom_3'=2] {'dom_2'}, use_global_device_ids=true, to_apply=%region_43.46 | all-reduce | flops 2 | bytes 16 | tf_op jit(solution)/shard_map/psum | solution.py:20
  395.1 10.0 %all-reduce.9 = (f32[]{:T(128)}, f32[]{:T(128)}) all-reduce(f32[]{:T(128)} %get-tuple-element.25, f32[]{:T(128)} %get-tuple-element.26), channel_id=1, replica_groups=mesh['dom_0'=4,'dom_1'=4,'dom_2'=4,'dom_3'=2] {'dom_3'}, use_global_device_ids=true, to_apply=%region_44.47 | all-reduce | flops 2 | bytes 16 | tf_op jit(solution)/shard_map/psum | solution.py:20
  (133 shorter events, 94.6 us)
Async XLA Ops:
  6.7 68.0 %all-to-all-start.1 = ((s32[128,1,8]{2,1,0:T(1,128)}), s32[128,1,8]{2,1,0:T(1,128)S(1)}, u32[]{:S(2)}, u32[]{:S(2)}) async-start(s32[128,1,8]{2,1,0:T(1,128)} %bitcast.41), calls=%async_computation.1 | async-start | bytes 131072 | tf_op jit(solution)/shard_map/all_to_all | solution.py:77
  74.7 9.9 %copy-start.4 = (f32[3,32,128]{2,1,0:T(8,128)S(1)}, f32[3,32,128]{2,1,0:T(8,128)}, u32[]{:S(2)}) copy-start(f32[3,32,128]{2,1,0:T(8,128)} %param.15) | copy-start | bytes 147460
  74.7 10.0 %copy-start.6 = (s32[16]{0:T(128)S(1)}, s32[16]{0:T(128)}, u32[]{:S(2)}) copy-start(s32[16]{0:T(128)} %param.20) | copy-start | bytes 196
  74.7 10.1 %copy-start.5 = (s32[2,128]{1,0:T(2,128)S(1)}, s32[2,128]{1,0:T(2,128)}, u32[]{:S(2)}) copy-start(s32[2,128]{1,0:T(2,128)} %param.19) | copy-start | bytes 3076
  74.7 51.6 %all-to-all-start = ((f32[128,8,6,128]{3,1,2,0:T(8,128)}), f32[128,8,6,128]{3,1,2,0:T(8,128)S(1)}, u32[]{:S(2)}, u32[]{:S(2)}) async-start(f32[128,8,6,128]{3,1,2,0:T(8,128)} %copy.104), calls=%async_computation | async-start | bytes 6291456 | tf_op jit(solution)/shard_map/all_to_all | solution.py:76
  126.3 2.2 copy-start.1
  126.3 2.2 copy-start.2
  126.3 2.2 copy-start.3
  172.2 176.4 %copy-start = (f32[96,128]{1,0:T(8,128)}, f32[96,128]{1,0:T(8,128)S(1)}, u32[]{:S(2)}) copy-start(f32[96,128]{1,0:T(8,128)S(1)} %fusion.41) | copy-start | bytes 147460
  176.1 5.6 %collective-permute-start.1 = (f32[96,16]{0,1:T(8,128)S(1)}, f32[96,16]{0,1:T(8,128)S(1)}, u32[]{:S(2)}, u32[]{:S(2)}) collective-permute-start(f32[96,16]{0,1:T(8,128)S(1)} %select_bitcast_fusion.3), channel_id=1, source_target_pairs={{1,0},{2,1},{3,2},{4,3},{5,4},{6,5},{7,6},{8,7},{9,8},{10,9},{11,1... | collective-permute-start | bytes 18440 | tf_op jit(solution)/shard_map/ppermute | solution.py:15
  179.2 3.3 collective-permute-start
  232.5 6.0 %collective-permute-start.3 = (f32[96,16]{0,1:T(8,128)S(1)}, f32[96,16]{0,1:T(8,128)S(1)}, u32[]{:S(2)}, u32[]{:S(2)}) collective-permute-start(f32[96,16]{0,1:T(8,128)S(1)} %select_bitcast_fusion.2), channel_id=1, source_target_pairs={{1,0},{2,1},{3,2},{4,3},{5,4},{6,5},{7,6},{8,7},{9,8},{10,9},{11,1... | collective-permute-start | bytes 18440 | tf_op jit(solution)/shard_map/ppermute | solution.py:15
  234.8 4.3 %collective-permute-start.2 = (f32[96,16]{0,1:T(8,128)S(1)}, f32[96,16]{0,1:T(8,128)S(1)}, u32[]{:S(2)}, u32[]{:S(2)}) collective-permute-start(f32[96,16]{0,1:T(8,128)S(1)} %select_bitcast_fusion.2), channel_id=1, source_target_pairs={{0,1},{1,2},{2,3},{3,4},{4,5},{5,6},{6,7},{7,8},{8,9},{9,10},{10,1... | collective-permute-start | bytes 18440 | tf_op jit(solution)/shard_map/ppermute | solution.py:15
  295.2 5.8 %collective-permute-start.5 = (f32[96,16]{0,1:T(8,128)S(1)}, f32[96,16]{0,1:T(8,128)S(1)}, u32[]{:S(2)}, u32[]{:S(2)}) collective-permute-start(f32[96,16]{0,1:T(8,128)S(1)} %select_bitcast_fusion.1), channel_id=1, source_target_pairs={{1,0},{2,1},{3,2},{4,3},{5,4},{6,5},{7,6},{8,7},{9,8},{10,9},{11,1... | collective-permute-start | bytes 18440 | tf_op jit(solution)/shard_map/ppermute | solution.py:15
  297.5 4.3 %collective-permute-start.4 = (f32[96,16]{0,1:T(8,128)S(1)}, f32[96,16]{0,1:T(8,128)S(1)}, u32[]{:S(2)}, u32[]{:S(2)}) collective-permute-start(f32[96,16]{0,1:T(8,128)S(1)} %select_bitcast_fusion.1), channel_id=1, source_target_pairs={{0,1},{1,2},{2,3},{3,4},{4,5},{5,6},{6,7},{7,8},{8,9},{9,10},{10,1... | collective-permute-start | bytes 18440 | tf_op jit(solution)/shard_map/ppermute | solution.py:15
  352.5 5.8 %collective-permute-start.7 = (f32[96,16]{0,1:T(8,128)S(1)}, f32[96,16]{0,1:T(8,128)S(1)}, u32[]{:S(2)}, u32[]{:S(2)}) collective-permute-start(f32[96,16]{0,1:T(8,128)S(1)} %select_bitcast_fusion), channel_id=1, source_target_pairs={{1,0},{2,1},{3,2},{4,3},{5,4},{6,5},{7,6},{8,7},{9,8},{10,9},{11,1... | collective-permute-start | bytes 18440 | tf_op jit(solution)/shard_map/ppermute | solution.py:15
  354.8 4.3 %collective-permute-start.6 = (f32[96,16]{0,1:T(8,128)S(1)}, f32[96,16]{0,1:T(8,128)S(1)}, u32[]{:S(2)}, u32[]{:S(2)}) collective-permute-start(f32[96,16]{0,1:T(8,128)S(1)} %select_bitcast_fusion), channel_id=1, source_target_pairs={{0,1},{1,2},{2,3},{3,4},{4,5},{5,6},{6,7},{7,8},{8,9},{9,10},{10,1... | collective-permute-start | bytes 18440 | tf_op jit(solution)/shard_map/ppermute | solution.py:15
where the time goes:
time: 410 us; the launch traced here: 408 us
  blocking collectives  148 us (36%)
  local copies, waits for them, and re-layouts  83.5 us (20%)
  other arithmetic  52.8 us (13%)
  starting transfers between devices  44.4 us (11%)
  matrix products  43.1 us (11%)
  waiting for transfers between devices  25.2 us (6%)
  between operations  10.3 us (3%)
    psum x16, blocking collectives, over_axes(): shard = lax.psum(shard, axis)  148 us
    scatter x1, local copies, waits for them, and re-layouts, on_device(): jnp.zeros((partitions * capacity, 6, node_count), jnp.float32)  47.3 us
    dot_general x1, matrix products, wendland_map(): jnp.einsum('bjn,bcn->bcj', weight, force, precision=lax.Precision.HIGHEST)  42.6 us
    dot_general x4, other arithmetic, apply_operator(): jnp.einsum('abi,bi->ai', blocks[neighbor + 1], taken, precision=lax.Preci...  24.9 us
    ppermute x8, starting transfers between devices, from_behind(): return lax.ppermute(block, axis, route)  23.1 us
    all_to_all x1, waiting for transfers between devices, on_device(): lax.all_to_all(outgoing, DOM, split_axis=0, concat_axis=0, tiled=True)  22.7 us
    dot_general x4, other arithmetic, precondition(): jnp.einsum('abi,bi->ai', precond, vector, precision=lax.Precision.HIGHEST)  12.5 us
    all_to_all x1, starting transfers between devices, on_device(): lax.all_to_all(slot_target, DOM, split_axis=0, concat_axis=0, tiled=True)  11.5 us
  transfers between devices with their start and end apart: 10, of which 5 were waited for; matrix products, arithmetic and copies ran while one was open for 19% of the time, Pallas kernels for 0%

commit v1 on v0

--- a/solution.py
+++ b/solution.py
@@ -17,7 +17,7 @@
 
 def over_axes(shard, axes):
     for axis in axes:
-        shard = lax.psum(shard, axis)
+        shard = jnp.sum(lax.all_gather(shard, axis), axis=0)
     return shard
 
 

time: 410 us -> 474 us (1.16)
  local copies, waits for them, and re-layouts: 83.5 us -> 134 us
  other arithmetic: 52.8 us -> 76.2 us
  blocking collectives: 148 us -> 138 us
    psum x16 -> x0, blocking collectives: 148 us -> none  [over_axes(): shard = lax.psum(shard, axis)]
    unnamed x0 -> x16, blocking collectives: none -> 138 us
    unnamed x24 -> x114, local copies, waits for them, and re-layouts: 0.82 us -> 52.6 us
    reduce_sum x0 -> x36, other arithmetic: none -> 22.3 us  [over_axes(): shard = jnp.sum(lax.all_gather(shard, axis), axis=0)]
  transfers between devices with their start and end apart: 10 -> 10, of which waited for: 5 -> 4; matrix products, arithmetic and copies ran while one was open for 19% -> 16% of each run, Pallas kernels for 0% -> 0%
where the time goes in v1:
time: 474 us; the launch traced here: 471 us
  blocking collectives  138 us (29%)
  local copies, waits for them, and re-layouts  134 us (28%)
  other arithmetic  76.2 us (16%)
  starting transfers between devices  44.5 us (9%)
  matrix products  43.1 us (9%)
  waiting for transfers between devices  24.3 us (5%)
  between operations  10.5 us (2%)
    unnamed x16, blocking collectives  138 us
    unnamed x114, local copies, waits for them, and re-layouts  52.6 us
    scatter x1, local copies, waits for them, and re-layouts, on_device(): jnp.zeros((partitions * capacity, 6, node_count), jnp.float32)  47.3 us
    dot_general x1, matrix products, wendland_map(): jnp.einsum('bjn,bcn->bcj', weight, force, precision=lax.Precision.HIGHEST)  42.6 us
    dot_general x4, other arithmetic, apply_operator(): jnp.einsum('abi,bi->ai', blocks[neighbor + 1], taken, precision=lax.Preci...  24.9 us
    ppermute x8, starting transfers between devices, from_behind(): return lax.ppermute(block, axis, route)  23.1 us
    all_to_all x1, waiting for transfers between devices, on_device(): lax.all_to_all(outgoing, DOM, split_axis=0, concat_axis=0, tiled=True)  22.5 us
    reduce_sum x36, other arithmetic, over_axes(): shard = jnp.sum(lax.all_gather(shard, axis), axis=0)  22.3 us
  transfers between devices with their start and end apart: 10, of which 4 were waited for; matrix products, arithmetic and copies ran while one was open for 16% of the time, Pallas kernels for 0%

profile of v1, /device:TPU:1, one launch (start us, length us, event | category | flops | bytes accessed | tf_op | source)
XLA Modules:
  0.0 471.0 jit_solution(5969502576382814308)
XLA Ops:
  6.7 11.5 %all-to-all-start.1 = ((s32[128,1,8]{2,1,0:T(1,128)}), s32[128,1,8]{2,1,0:T(1,128)S(1)}, u32[]{:S(2)}, u32[]{:S(2)}) async-start(s32[128,1,8]{2,1,0:T(1,128)} %bitcast.41), calls=%async_computation.1 | async-start | bytes 131072 | tf_op jit(solution)/shard_map/all_to_all | solution.py:77
  22.8 47.3 %scatter_fusion = f32[1024,6,128]{2,1,0:T(8,128)} fusion(f32[1024,6,128]{2,1,0:T(8,128)} %broadcast_in_dim.40, s32[512]{0:T(512)S(1)} %bitcast.289, f32[512,6,128]{2,1,0:T(8,128)S(1)} %copy.103), kind=kCustom, calls=%fused_computation.13 | custom fusion | bytes 4720640 | tf_op jit(solution)/shard_map/scatter | solution.py:73
  74.7 9.8 %all-to-all-start = ((f32[128,8,6,128]{3,1,2,0:T(8,128)}), f32[128,8,6,128]{3,1,2,0:T(8,128)S(1)}, u32[]{:S(2)}, u32[]{:S(2)}) async-start(f32[128,8,6,128]{3,1,2,0:T(8,128)} %copy.104), calls=%async_computation | async-start | bytes 6291456 | tf_op jit(solution)/shard_map/all_to_all | solution.py:76
  87.9 8.0 %gather_fusion = f32[1024,3,32]{2,1,0:T(4,128)} fusion(f32[3,32,128]{1,0,2:T(4,128)S(1)} %copy.107, s32[1024]{0:T(1024)S(1)} %broadcast_clamp_fusion), kind=kCustom, calls=%fused_computation.12 | custom fusion | bytes 790528 | tf_op jit(solution)/shard_map/jit(_take)/gather | solution.py:80
  103.7 22.5 %all-to-all-done = f32[128,8,6,128]{3,1,2,0:T(8,128)S(1)} async-done(((f32[128,8,6,128]{3,1,2,0:T(8,128)}), f32[128,8,6,128]{3,1,2,0:T(8,128)S(1)}, u32[]{:S(2)}, u32[]{:S(2)}) %all-to-all-start) | async-done | bytes 3145760 | tf_op jit(solution)/shard_map/all_to_all | solution.py:76
  128.5 42.6 %fusion = f32[1024,3,32]{2,1,0:T(4,128)S(1)} fusion(f32[1024,128]{1,0:T(8,128)S(1)} %bitcast.282, f32[1024,32]{1,0:T(8,128)S(1)} %bitcast.280, f32[1024,128]{1,0:T(8,128)S(1)} %bitcast.283, f32[1024,32]{1,0:T(8,128)S(1)} %bitcast.279, f32[1024,128]{1,0:T(8,128)S(1)} %bitcast.281, f32[1024,32]{1,0:T(8,128)S(1)} %bitcast.278, f32[1024,6,128]{2,1,0:T(8,128)S(1)} %bitcast.263), kind=kOutput, calls=%fused_computation.15 | convolution fusion | flops 218103808 | bytes 5636096 | tf_op jit(solution)/shard_map/bjn,bcn->bcj/dot_general | solution.py:32
  184.5 6.2 %fusion.32 = (f32[128,96]{0,1:T(8,128)S(1)}, f32[128,96]{0,1:T(8,128)S(1)}, f32[128,96]{0,1:T(8,128)S(1)}) fusion(f32[3,96,96,128]{3,2,1,0:T(8,128)} %param.18, f32[128,96]{0,1:T(8,128)S(1)} %copy.236, f32[128,96]{0,1:T(8,128)S(1)} %multiply_reduce_fusion.3, f32[128,96]{0,1:T(8,128)S(1)} %copy.237), kind=kLoop, calls=%fused_computation.55 | loop fusion | flops 7041024 | bytes 14450688 | tf_op jit(solution)/shard_map/abi,bi->ai/dot_general | solution.py:48
  194.8 7.3 %all-reduce.44 = (f32[4]{0:T(128)S(1)}, f32[4]{0:T(128)S(1)}) all-reduce(f32[4]{0:T(128)S(1)} %dynamic-update-slice, f32[4]{0:T(128)S(1)} %dynamic-update-slice.4), channel_id=1, replica_groups=mesh['dom_0'=4,'dom_1'=4,'dom_2'=4,'dom_3'=2] {'dom_0'}, use_global_device_ids=true, to_apply=%add | all-reduce | flops 8 | bytes 64
  217.1 10.5 %all-reduce.38 = (f32[4]{0:T(128)S(1)}, f32[4]{0:T(128)S(1)}) all-reduce(f32[4]{0:T(128)S(1)} %dynamic-update-slice.2, f32[4]{0:T(128)S(1)} %dynamic-update-slice.6), channel_id=1, replica_groups=mesh['dom_0'=4,'dom_1'=4,'dom_2'=4,'dom_3'=2] {'dom_2'}, use_global_device_ids=true, to_apply=%add.2 | all-reduce | flops 8 | bytes 64
  231.6 9.9 %all-reduce.47 = (f32[2]{0:T(128)S(1)}, f32[2]{0:T(128)S(1)}) all-reduce(f32[2]{0:T(128)S(1)} %dynamic-update-slice.3, f32[2]{0:T(128)S(1)} %dynamic-update-slice.7), channel_id=1, replica_groups=mesh['dom_0'=4,'dom_1'=4,'dom_2'=4,'dom_3'=2] {'dom_3'}, use_global_device_ids=true, to_apply=%add.3 | all-reduce | flops 4 | bytes 32
  256.5 6.2 %fusion.33 = (f32[128,96]{0,1:T(8,128)S(1)}, f32[128,96]{0,1:T(8,128)S(1)}, f32[128,96]{0,1:T(8,128)S(1)}) fusion(f32[3,96,96,128]{3,2,1,0:T(8,128)} %param.18, f32[128,96]{0,1:T(8,128)S(1)} %copy.241, f32[128,96]{0,1:T(8,128)S(1)} %multiply_reduce_fusion.2, f32[128,96]{0,1:T(8,128)S(1)} %copy.242), kind=kLoop, calls=%fused_computation.56 | loop fusion | flops 7041024 | bytes 14450688 | tf_op jit(solution)/shard_map/abi,bi->ai/dot_general | solution.py:48
  269.1 8.6 %all-reduce.43 = (f32[4]{0:T(128)S(1)}, f32[4]{0:T(128)S(1)}, f32[4]{0:T(128)S(1)}, f32[4]{0:T(128)S(1)}) all-reduce(f32[4]{0:T(128)S(1)} %dynamic-update-slice.16, f32[4]{0:T(128)S(1)} %dynamic-update-slice.8, f32[4]{0:T(128)S(1)} %dynamic-update-slice.12, ...), channel_id=1, replica_groups=mesh['dom_0'=4,'dom_1'=4,'dom_2'=4,'dom_3'=2] {'dom_0'}, use_global_device_ids=true, to_apply=%add.16 | all-reduce | flops 16 | bytes 128
  285.8 6.0 %all-reduce.40 = (f32[4]{0:T(128)S(1)}, f32[4]{0:T(128)S(1)}, f32[4]{0:T(128)S(1)}, f32[4]{0:T(128)S(1)}) all-reduce(f32[4]{0:T(128)S(1)} %dynamic-update-slice.17, f32[4]{0:T(128)S(1)} %dynamic-update-slice.9, f32[4]{0:T(128)S(1)} %dynamic-update-slice.13, ...), channel_id=1, replica_groups=mesh['dom_0'=4,'dom_1'=4,'dom_2'=4,'dom_3'=2] {'dom_1'}, use_global_device_ids=true, to_apply=%add.17 | all-reduce | flops 16 | bytes 128
  299.4 10.8 %all-reduce.37 = (f32[4]{0:T(128)S(1)}, f32[4]{0:T(128)S(1)}, f32[4]{0:T(128)S(1)}, f32[4]{0:T(128)S(1)}) all-reduce(f32[4]{0:T(128)S(1)} %dynamic-update-slice.18, f32[4]{0:T(128)S(1)} %dynamic-update-slice.10, f32[4]{0:T(128)S(1)} %dynamic-update-slice.14, ...), channel_id=1, replica_groups=mesh['dom_0'=4,'dom_1'=4,'dom_2'=4,'dom_3'=2] {'dom_2'}, use_global_device_ids=true, to_apply=%add.18 | all-reduce | flops 16 | bytes 128
  318.1 9.4 %all-reduce.46 = (f32[2]{0:T(128)S(1)}, f32[2]{0:T(128)S(1)}, f32[2]{0:T(128)S(1)}, f32[2]{0:T(128)S(1)}) all-reduce(f32[2]{0:T(128)S(1)} %dynamic-update-slice.19, f32[2]{0:T(128)S(1)} %dynamic-update-slice.11, f32[2]{0:T(128)S(1)} %dynamic-update-slice.15, ...), channel_id=1, replica_groups=mesh['dom_0'=4,'dom_1'=4,'dom_2'=4,'dom_3'=2] {'dom_3'}, use_global_device_ids=true, to_apply=%add.19 | all-reduce | flops 8 | bytes 64
  348.2 6.2 %fusion.34 = (f32[128,96]{0,1:T(8,128)S(1)}, f32[128,96]{0,1:T(8,128)S(1)}, f32[128,96]{0,1:T(8,128)S(1)}) fusion(f32[3,96,96,128]{3,2,1,0:T(8,128)} %param.18, f32[128,96]{0,1:T(8,128)S(1)} %copy.246, f32[128,96]{0,1:T(8,128)S(1)} %multiply_reduce_fusion.1, f32[128,96]{0,1:T(8,128)S(1)} %copy.247), kind=kLoop, calls=%fused_computation.57 | loop fusion | flops 7041024 | bytes 14450688 | tf_op jit(solution)/shard_map/abi,bi->ai/dot_general | solution.py:48
  356.5 8.6 %all-reduce.24 = f32[4]{0:T(128)S(1)} all-reduce(f32[4]{0:T(128)S(1)} %dynamic-update-slice.24), channel_id=1, replica_groups=mesh['dom_0'=4,'dom_1'=4,'dom_2'=4,'dom_3'=2] {'dom_0'}, use_global_device_ids=true, to_apply=%add.24 | all-reduce | flops 4 | bytes 32
  367.1 6.2 %all-reduce.25 = f32[4]{0:T(128)S(1)} all-reduce(f32[4]{0:T(128)S(1)} %dynamic-update-slice.25), channel_id=1, replica_groups=mesh['dom_0'=4,'dom_1'=4,'dom_2'=4,'dom_3'=2] {'dom_1'}, use_global_device_ids=true, to_apply=%add.25 | all-reduce | flops 4 | bytes 32
  375.3 10.5 %all-reduce.26 = f32[4]{0:T(128)S(1)} all-reduce(f32[4]{0:T(128)S(1)} %dynamic-update-slice.26), channel_id=1, replica_groups=mesh['dom_0'=4,'dom_1'=4,'dom_2'=4,'dom_3'=2] {'dom_2'}, use_global_device_ids=true, to_apply=%add.26 | all-reduce | flops 4 | bytes 32
  387.8 9.4 %all-reduce.27 = f32[2]{0:T(128)S(1)} all-reduce(f32[2]{0:T(128)S(1)} %dynamic-update-slice.27), channel_id=1, replica_groups=mesh['dom_0'=4,'dom_1'=4,'dom_2'=4,'dom_3'=2] {'dom_3'}, use_global_device_ids=true, to_apply=%add.27 | all-reduce | flops 2 | bytes 16
  410.8 6.2 %fusion.35 = (f32[128,96]{0,1:T(8,128)S(1)}, f32[128,96]{0,1:T(8,128)S(1)}, f32[128,96]{0,1:T(8,128)S(1)}) fusion(f32[3,96,96,128]{3,2,1,0:T(8,128)} %param.18, f32[128,96]{0,1:T(8,128)S(1)} %copy.251, f32[128,96]{0,1:T(8,128)S(1)} %multiply_reduce_fusion, f32[128,96]{0,1:T(8,128)S(1)} %copy.252), kind=kLoop, calls=%fused_computation.58 | loop fusion | flops 7041024 | bytes 14450688 | tf_op jit(solution)/shard_map/abi,bi->ai/dot_general | solution.py:48
  420.6 8.6 %all-reduce.42 = (f32[4]{0:T(128)S(1)}, f32[4]{0:T(128)S(1)}) all-reduce(f32[4]{0:T(128)S(1)} %dynamic-update-slice.28, f32[4]{0:T(128)S(1)} %dynamic-update-slice.32), channel_id=1, replica_groups=mesh['dom_0'=4,'dom_1'=4,'dom_2'=4,'dom_3'=2] {'dom_0'}, use_global_device_ids=true, to_apply=%add.28 | all-reduce | flops 8 | bytes 64
  443.0 10.8 %all-reduce.36 = (f32[4]{0:T(128)S(1)}, f32[4]{0:T(128)S(1)}) all-reduce(f32[4]{0:T(128)S(1)} %dynamic-update-slice.30, f32[4]{0:T(128)S(1)} %dynamic-update-slice.34), channel_id=1, replica_groups=mesh['dom_0'=4,'dom_1'=4,'dom_2'=4,'dom_3'=2] {'dom_2'}, use_global_device_ids=true, to_apply=%add.30 | all-reduce | flops 8 | bytes 64
  457.8 9.4 %all-reduce.45 = (f32[2]{0:T(128)S(1)}, f32[2]{0:T(128)S(1)}) all-reduce(f32[2]{0:T(128)S(1)} %dynamic-update-slice.31, f32[2]{0:T(128)S(1)} %dynamic-update-slice.35), channel_id=1, replica_groups=mesh['dom_0'=4,'dom_1'=4,'dom_2'=4,'dom_3'=2] {'dom_3'}, use_global_device_ids=true, to_apply=%add.31 | all-reduce | flops 4 | bytes 32
  (259 shorter events, 167.7 us)
Async XLA Ops:
  6.7 68.0 %all-to-all-start.1 = ((s32[128,1,8]{2,1,0:T(1,128)}), s32[128,1,8]{2,1,0:T(1,128)S(1)}, u32[]{:S(2)}, u32[]{:S(2)}) async-start(s32[128,1,8]{2,1,0:T(1,128)} %bitcast.41), calls=%async_computation.1 | async-start | bytes 131072 | tf_op jit(solution)/shard_map/all_to_all | solution.py:77
  74.7 9.9 %copy-start.4 = (f32[3,32,128]{2,1,0:T(8,128)S(1)}, f32[3,32,128]{2,1,0:T(8,128)}, u32[]{:S(2)}) copy-start(f32[3,32,128]{2,1,0:T(8,128)} %param.15) | copy-start | bytes 147460
  74.7 10.0 %copy-start.9 = (s32[16]{0:T(128)S(1)}, s32[16]{0:T(128)}, u32[]{:S(2)}) copy-start(s32[16]{0:T(128)} %param.20) | copy-start | bytes 196
  74.7 10.6 %copy-start.8 = (s32[2,128]{1,0:T(2,128)S(1)}, s32[2,128]{1,0:T(2,128)}, u32[]{:S(2)}) copy-start(s32[2,128]{1,0:T(2,128)} %param.19) | copy-start | bytes 3076
  74.7 51.6 %all-to-all-start = ((f32[128,8,6,128]{3,1,2,0:T(8,128)}), f32[128,8,6,128]{3,1,2,0:T(8,128)S(1)}, u32[]{:S(2)}, u32[]{:S(2)}) async-start(f32[128,8,6,128]{3,1,2,0:T(8,128)} %copy.104), calls=%async_computation | async-start | bytes 6291456 | tf_op jit(solution)/shard_map/all_to_all | solution.py:76
  126.3 2.2 copy-start.1
  126.3 2.2 copy-start.2
  126.3 2.2 copy-start.3
  171.1 4.4 copy-start.5
  171.1 5.0 %copy-start.6 = (pred[16]{0:T(512)(128)(4,1)S(1)}, pred[16]{0:T(512)(128)(4,1)}, u32[]{:S(2)}) copy-start(pred[16]{0:T(512)(128)(4,1)} %compare_and_fusion.3) | copy-start | bytes 52
  171.1 10.6 %copy-start.7 = (s32[128]{0:T(128)S(1)}, s32[128]{0:T(128)}, u32[]{:S(2)}) copy-start(s32[128]{0:T(128)} %get-tuple-element.61) | copy-start | bytes 1540
  171.1 10.6 %copy-start.13 = (u32[128]{0:T(128)S(1)}, u32[128]{0:T(128)}, u32[]{:S(2)}) copy-start(u32[128]{0:T(128)} %constant.62) | copy-start | bytes 1540
  172.3 226.2 %copy-start = (f32[96,128]{1,0:T(8,128)}, f32[96,128]{1,0:T(8,128)S(1)}, u32[]{:S(2)}) copy-start(f32[96,128]{1,0:T(8,128)S(1)} %fusion.41) | copy-start | bytes 147460
  176.2 6.3 %collective-permute-start.1 = (f32[96,16]{0,1:T(8,128)S(1)}, f32[96,16]{0,1:T(8,128)S(1)}, u32[]{:S(2)}, u32[]{:S(2)}) collective-permute-start(f32[96,16]{0,1:T(8,128)S(1)} %select_bitcast_fusion.3), channel_id=1, source_target_pairs={{1,0},{2,1},{3,2},{4,3},{5,4},{6,5},{7,6},{8,7},{9,8},{10,9},{11,1... | collective-permute-start | bytes 18440 | tf_op jit(solution)/shard_map/ppermute | solution.py:15
  179.2 3.3 collective-permute-start
  184.5 9.8 %copy-start.12 = (u32[128]{0:T(128)S(1)}, u32[128]{0:T(128)}, u32[]{:S(2)}) copy-start(u32[128]{0:T(128)} %constant.67) | copy-start | bytes 1540
  184.5 21.6 %copy-start.11 = (u32[128]{0:T(128)S(1)}, u32[128]{0:T(128)}, u32[]{:S(2)}) copy-start(u32[128]{0:T(128)} %constant.72) | copy-start | bytes 1540
  184.5 32.0 %copy-start.10 = (u32[128]{0:T(128)S(1)}, u32[128]{0:T(128)}, u32[]{:S(2)}) copy-start(u32[128]{0:T(128)} %constant.77) | copy-start | bytes 1540
  248.0 5.8 %collective-permute-start.3 = (f32[96,16]{0,1:T(8,128)S(1)}, f32[96,16]{0,1:T(8,128)S(1)}, u32[]{:S(2)}, u32[]{:S(2)}) collective-permute-start(f32[96,16]{0,1:T(8,128)S(1)} %select_bitcast_fusion.2), channel_id=1, source_target_pairs={{1,0},{2,1},{3,2},{4,3},{5,4},{6,5},{7,6},{8,7},{9,8},{10,9},{11,1... | collective-permute-start | bytes 18440 | tf_op jit(solution)/shard_map/ppermute | solution.py:15
  250.3 4.3 collective-permute-start.2
  339.7 5.8 %collective-permute-start.5 = (f32[96,16]{0,1:T(8,128)S(1)}, f32[96,16]{0,1:T(8,128)S(1)}, u32[]{:S(2)}, u32[]{:S(2)}) collective-permute-start(f32[96,16]{0,1:T(8,128)S(1)} %select_bitcast_fusion.1), channel_id=1, source_target_pairs={{1,0},{2,1},{3,2},{4,3},{5,4},{6,5},{7,6},{8,7},{9,8},{10,9},{11,1... | collective-permute-start | bytes 18440 | tf_op jit(solution)/shard_map/ppermute | solution.py:15
  341.9 4.3 collective-permute-start.4
  402.4 6.1 %collective-permute-start.7 = (f32[96,16]{0,1:T(8,128)S(1)}, f32[96,16]{0,1:T(8,128)S(1)}, u32[]{:S(2)}, u32[]{:S(2)}) collective-permute-start(f32[96,16]{0,1:T(8,128)S(1)} %select_bitcast_fusion), channel_id=1, source_target_pairs={{1,0},{2,1},{3,2},{4,3},{5,4},{6,5},{7,6},{8,7},{9,8},{10,9},{11,1... | collective-permute-start | bytes 18440 | tf_op jit(solution)/shard_map/ppermute | solution.py:15
  404.6 4.3 collective-permute-start.6
